TPU v7x, 128 devices: a whole 4x4x4 slice. The times are simulated.
128 devices in a mesh: dp: 16 (over z, x), tensor: 8 (over y, core).
Axes of the slice: x: 4, y: 4, z: 4, core: 2. Of those that a mesh axis runs over, the one named last changes fastest.
Arguments:
- tokens: bfloat16 [128, 128, 8192], P('dp', None, 'tensor'), may hold values from -6 to 6
- shared_prefix_tokens: bfloat16 [16, 256, 8192], P('dp', None, 'tensor'), may hold values from -6 to 6
- input_norm_gain: bfloat16 [8192], replicated, may hold values from 0.5 to 8
- query_weight: bfloat16 [8192, 8192], P(None, 'tensor'), may hold values from -0.0625 to 0.0625
- key_weight: bfloat16 [8192, 1024], P(None, 'tensor'), may hold values from -0.0625 to 0.0625
- value_weight: bfloat16 [8192, 1024], P(None, 'tensor'), may hold values from -0.0625 to 0.0625
- adapter_down_weight: bfloat16 [64, 8192, 16], P('dp', 'tensor'), may hold values from -0.0625 to 0.0625
- adapter_up_weight: bfloat16 [64, 16, 8192], P('dp', None, 'tensor'), may hold values from -0.75 to 0.75
- adapter_position: int32 [64], replicated, may hold values from 0 to 63, as said below
- request_adapter: int32 [128], P('dp'), may hold values from 0 to 63, as said below
- request_group: int32 [128], P('dp'), may hold values from 0 to 15
- lengths: int32 [128], P('dp'), may hold values from 1 to 128
- request_page_table: int32 [128, 1], P('dp'), may hold values from 0 to 127, as said below
Outputs:
- context: bfloat16 [128, 128, 8192], P('dp', None, 'tensor')
- paged_key_values: bfloat16 [128, 2, 128, 1024], P('dp', None, None, 'tensor')
Inputs may be any that keep to these rules, and one draw needn't show every extreme that they name: A permutation: adapter a is held at slot adapter_position[a], on index adapter_position[a] // 4 of dp. `request_adapter`: the 8 requests of one index of dp use adapters held by 8 different indices of dp. `request_page_table`: the requests of index i of dp use the pages i * 8 to (i + 1) * 8 - 1, each page once.
All inputs are finite; a program needn't handle non-finite values.
Results may differ from a plain program's by a relative error of at most 0.011.
The roundings to bfloat16 on the way count: a program that leaves them out, or rounds other values in their place, can miss the bound.
Values may be sent and summed in bfloat16 or wider, within the bound.
No kernel may reach another device: no remote copies, remote signals or barrier semaphores. Data moves between devices by JAX's collectives and lax.ppermute only.
A program may use at most 128 MiB of HBM per device.

v0:
```python
import jax
import jax.numpy as jnp
from jax import lax
from jax.sharding import PartitionSpec as P

HEAD_WIDTH = 128
ADAPTER_RANK = 16
PAGE_TOKENS = 128
EPS = 1e-05
THETA = 500000.0
ADAPTER_SCALE = 2.0


def rope_tables(positions, width):
    half = width // 2
    freq = THETA ** (-(jnp.arange(half, dtype=jnp.float32) * 2.0 / width))
    angle = positions.astype(jnp.float32)[:, None] * freq[None, :]
    return (jnp.cos(angle), jnp.sin(angle))


def apply_rope(values, cosine, sine):
    half = values.shape[-1] // 2
    first = values[..., :half]
    second = values[..., half:]
    cos_b = cosine[:, None, :]
    sin_b = sine[:, None, :]
    return jnp.concatenate(
        [first * cos_b - second * sin_b, second * cos_b + first * sin_b], axis=-1
    )


def normalize(rows, gain):
    values = rows.astype(jnp.float32)
    scale = lax.rsqrt(jnp.mean(values * values, axis=-1, keepdims=True) + EPS)
    return (values * scale * gain.astype(jnp.float32)).astype(jnp.bfloat16)


def on_device(
    tokens,
    shared_prefix_tokens,
    input_norm_gain,
    query_weight,
    key_weight,
    value_weight,
    adapter_down_weight,
    adapter_up_weight,
    adapter_position,
    request_adapter,
    request_group,
    lengths,
    request_page_table,
):
    req_dev, seq_len, d_part = tokens.shape
    grp_dev, pre_len, _ = shared_prefix_tokens.shape
    q_width = query_weight.shape[1]
    kv_width = key_weight.shape[1]
    q_heads = q_width // HEAD_WIDTH
    kv_local = kv_width // HEAD_WIDTH
    group_members = q_heads // kv_local
    token_rows = req_dev * seq_len
    column = lax.axis_index("tensor")
    place = lax.axis_index("dp")
    full_tokens, full_prefix = (
        lax.all_gather(tokens.reshape(token_rows, d_part), "tensor", axis=1, tiled=True),
        lax.all_gather(
            shared_prefix_tokens.reshape(grp_dev * pre_len, d_part), "tensor", axis=1, tiled=True
        ),
    )
    normed_input = normalize(full_tokens, input_norm_gain)
    prefix_normed = normalize(full_prefix, input_norm_gain)
    pre_cos, pre_sin = rope_tables(jnp.arange(pre_len), HEAD_WIDTH)
    pre_keys = jnp.dot(prefix_normed, key_weight, preferred_element_type=jnp.float32).reshape(
        grp_dev, pre_len, kv_local, HEAD_WIDTH
    )
    pre_keys = (
        apply_rope(pre_keys, pre_cos, pre_sin)
        .astype(jnp.bfloat16)
        .reshape(grp_dev, pre_len, kv_width)
    )
    pre_vals = (
        jnp.dot(prefix_normed, value_weight, preferred_element_type=jnp.float32)
        .astype(jnp.bfloat16)
        .reshape(grp_dev, pre_len, kv_width)
    )
    all_pairs = lax.all_gather(jnp.stack([pre_keys, pre_vals], 1), "dp", axis=0, tiled=True)
    table_ids = jnp.arange(adapter_position.shape[0])
    slots = jnp.sum(
        jnp.where(request_adapter[:, None] == table_ids[None, :], adapter_position[None, :], 0),
        axis=1,
    )
    local_rows = lax.dynamic_slice_in_dim(normed_input, column * d_part, d_part, 1)
    row_slot = jnp.repeat(slots, seq_len)
    page_piece = lax.all_gather(adapter_down_weight, "dp", axis=0, tiled=True)
    count = page_piece.shape[0]
    part = jnp.einsum("td,ndr->tnr", local_rows, page_piece, preferred_element_type=jnp.float32)
    pick = row_slot[:, None] == jnp.arange(count)[None, :]
    partial_low = jnp.sum(jnp.where(pick[:, :, None], part, 0.0), axis=1)
    low_rank_rows = lax.psum(partial_low, "tensor").astype(jnp.bfloat16)
    page_piece = lax.all_gather(adapter_up_weight, "dp", axis=0, tiled=True)
    count = page_piece.shape[0]
    pick = (row_slot[:, None] == jnp.arange(count)[None, :]).astype(jnp.bfloat16)
    spread = (pick[:, :, None] * low_rank_rows[:, None, :]).reshape(
        token_rows, count * ADAPTER_RANK
    )
    summed_rows = jnp.dot(
        spread,
        page_piece.reshape(count * ADAPTER_RANK, q_width),
        preferred_element_type=jnp.float32,
    )
    adapter_term = (ADAPTER_SCALE * summed_rows).astype(jnp.bfloat16)
    own_cos, own_sin = rope_tables(pre_len + jnp.arange(seq_len), HEAD_WIDTH)
    query_rows = jnp.dot(
        normed_input, query_weight, preferred_element_type=jnp.float32
    ) + adapter_term.astype(jnp.float32)
    query_rows = apply_rope(
        query_rows.reshape(req_dev, seq_len, q_heads, HEAD_WIDTH), own_cos, own_sin
    ).astype(jnp.bfloat16)
    key_rows = jnp.dot(normed_input, key_weight, preferred_element_type=jnp.float32).reshape(
        req_dev, seq_len, kv_local, HEAD_WIDTH
    )
    key_rows = apply_rope(key_rows, own_cos, own_sin).astype(jnp.bfloat16)
    value_rows = (
        jnp.dot(normed_input, value_weight, preferred_element_type=jnp.float32)
        .astype(jnp.bfloat16)
        .reshape(req_dev, seq_len, kv_local, HEAD_WIDTH)
    )
    live = jnp.arange(seq_len)[None, :] < lengths[:, None]
    key_rows = jnp.where(live[:, :, None, None], key_rows, jnp.zeros_like(key_rows))
    value_rows = jnp.where(live[:, :, None, None], value_rows, jnp.zeros_like(value_rows))
    chosen = all_pairs[request_group]
    all_keys = jnp.concatenate(
        [chosen[:, 0].reshape(req_dev, pre_len, kv_local, HEAD_WIDTH), key_rows], 1
    )
    all_vals = jnp.concatenate(
        [chosen[:, 1].reshape(req_dev, pre_len, kv_local, HEAD_WIDTH), value_rows], 1
    )
    grouped_query = query_rows.reshape(req_dev, seq_len, kv_local, group_members, HEAD_WIDTH)
    scores = jnp.einsum(
        "btkgd,bskd->bkgts", grouped_query, all_keys, preferred_element_type=jnp.float32
    ) * HEAD_WIDTH ** (-0.5)
    seen = jnp.arange(pre_len + seq_len)[None, :]
    allowed = (seen < pre_len) | (seen - pre_len <= jnp.arange(seq_len)[:, None])
    scores = jnp.where(allowed[None, None, None], scores, -1e30)
    top = jnp.max(scores, axis=-1, keepdims=True)
    weights = jnp.exp(scores - top)
    probs = (weights / jnp.sum(weights, axis=-1, keepdims=True)).astype(jnp.bfloat16)
    attention_output = jnp.einsum(
        "bkgts,bskd->btkgd", probs, all_vals, preferred_element_type=jnp.float32
    )
    attention_output = jnp.where(live[:, :, None, None, None], attention_output, 0.0)
    context = attention_output.reshape(req_dev, seq_len, q_width).astype(jnp.bfloat16)
    pages_req = seq_len // PAGE_TOKENS
    page_blocks = jnp.stack(
        [
            key_rows.reshape(req_dev, pages_req, PAGE_TOKENS, kv_width),
            value_rows.reshape(req_dev, pages_req, PAGE_TOKENS, kv_width),
        ],
        2,
    )
    page_blocks = page_blocks.reshape(req_dev * pages_req, 2, PAGE_TOKENS, kv_width)
    local_page = request_page_table.reshape(-1) - place * (req_dev * pages_req)
    paged_key_values = jnp.zeros_like(page_blocks).at[local_page].set(page_blocks)
    return (context, paged_key_values)


def solution(mesh):
    in_specs = (
        P("dp", None, "tensor"),
        P("dp", None, "tensor"),
        P(),
        P(None, "tensor"),
        P(None, "tensor"),
        P(None, "tensor"),
        P("dp", "tensor", None),
        P("dp", None, "tensor"),
        P(),
        P("dp"),
        P("dp"),
        P("dp"),
        P("dp", None),
    )
    out_specs = (P("dp", None, "tensor"), P("dp", None, None, "tensor"))
    return jax.shard_map(
        on_device, mesh=mesh, in_specs=in_specs, out_specs=out_specs, check_vma=False
    )
```

profile of v0, /device:TPU:0, one launch (start us, length us, event | category | flops | bytes accessed | tf_op | source)
XLA Modules:
  0.0 344.5 jit_solution(120121396503228455)
XLA Ops:
  7.2 0.0 copy-start
  7.2 0.0 all-gather.15.cloned.1.call-start
  7.2 0.7 all-gather.15.cloned.1.call-update
  7.9 0.0 all-gather.7.cloned.1.call-start
  8.0 0.7 convert_element_type.114
  8.7 35.6 %all-gather.15.cloned.1.call-done = bf16[1,256,8192]{2,1,0:T(8,128)(2,1)} async-done(((bf16[1,256,1024]{2,1,0:T(8,128)(2,1)}), bf16[1,256,8192]{2,1,0:T(8,128)(2,1)}) %all-gather.15.cloned.1.call-update) | async-done | bytes 4194320 | tf_op jit(solution)/shard_map/all_gather | solution.py:65
  44.3 3.3 fusion.5
  47.6 0.2 copy-done.4
  47.8 3.3 fusion.33
  51.1 0.3 fusion.58
  51.5 0.0 copy-start.13
  51.5 0.0 copy-start.14
  51.5 1.7 fusion.39
  53.3 0.8 copy.63
  54.1 0.0 all-gather.7.cloned.1.call-update
  54.1 0.0 all-gather.9.cloned.1.call-start
  54.1 0.7 all-gather.9.cloned.1.call-update
  54.8 0.0 all-gather.11.cloned.1.call-start
  54.9 0.5 all-gather.11.cloned.1.call-update
  55.4 0.0 all-gather.13.cloned.1.call-start
  55.4 0.5 all-gather.13.cloned.1.call-update
  56.0 0.2 select_reduce_fusion.1
  56.2 0.1 broadcast_bitcast_fusion
  56.3 0.1 fusion.65
  56.4 0.3 multiply_cosine_fusion
  56.7 0.6 iota_compare_fusion.3
  57.3 0.6 pad_clamp_fusion
  57.9 0.2 fusion.48
  58.1 0.5 fusion.59
  58.6 40.8 %all-gather.7.cloned.1.call-done = bf16[16,2,256,128]{3,2,1,0:T(8,128)(2,1)} async-done(((bf16[1,2,256,128]{3,2,1,0:T(8,128)(2,1)}), bf16[16,2,256,128]{3,2,1,0:T(8,128)(2,1)}) %all-gather.7.cloned.1.call-update) | async-done | bytes 2097168 | tf_op jit(solution)/shard_map/all_gather | solution.py:85
  99.4 2.5 gather_fusion
  101.9 1.0 fusion.67
  102.9 2.0 copy.78
  105.0 80.4 %all-gather.9.cloned.1.call-done = bf16[1024,8192]{1,0:T(8,128)(2,1)} async-done(((bf16[1024,1024]{1,0:T(8,128)(2,1)}), bf16[1024,8192]{1,0:T(8,128)(2,1)}) %all-gather.9.cloned.1.call-update) | async-done | bytes 16777232 | tf_op jit(solution)/shard_map/all_gather | solution.py:64
  185.4 7.5 %fusion = f32[1024]{0:T(1024)S(1)} fusion(bf16[1024,8192]{1,0:T(8,128)(2,1)} %all-gather.9.cloned.1.call-done), kind=kLoop, calls=%fused_computation.4 | loop fusion | flops 25164800 | bytes 16781312 | tf_op jit(solution)/shard_map/reduce_sum | solution.py:34
  192.9 3.2 copy-done.2
  196.0 8.3 %fusion.2 = bf16[1024,8192]{1,0:T(8,128)(2,1)} fusion(bf16[1024,8192]{1,0:T(8,128)(2,1)S(1)} %copy-done.2, f32[8192]{0:T(1024)S(1)} %convert_element_type.114, f32[1024]{0:T(1024)S(1)} %add_rsqrt_fusion), kind=kLoop, calls=%fused_computation.6 | loop fusion | flops 33554432 | bytes 33591296 | tf_op jit(solution)/shard_map/convert_element_type | solution.py:35
  204.3 29.0 %all-gather.11.cloned.1.call-done = bf16[64,1024,16]{1,2,0:T(8,128)(2,1)} async-done(((bf16[4,1024,16]{1,2,0:T(8,128)(2,1)}), bf16[64,1024,16]{1,2,0:T(8,128)(2,1)}) %all-gather.11.cloned.1.call-update) | async-done | bytes 2097168 | tf_op jit(solution)/shard_map/all_gather | solution.py:93
  233.3 5.1 %select_reduce_fusion = f32[1024,16]{0,1:T(8,128)S(1)} fusion(pred[1024,64]{0,1:T(8,128)(4,1)S(1)} %get-tuple-element.23, bf16[64,1024,16]{1,2,0:T(8,128)(2,1)} %all-gather.11.cloned.1.call-done, bf16[1024,8192]{1,0:T(8,128)(2,1)} %fusion.2, s32[]{:T(128)S(6)} %select_n.72), kind=kOutput, calls=%fused_computation.27 | convolution fusion | flops 2149564416 | bytes 4325380 | tf_op jit(solution)/shard_map/td,ndr->tnr/dot_general | solution.py:95
  238.4 25.3 %psum.7 = bf16[1024,16]{0,1:T(8,128)(2,1)S(1)} all-reduce(f32[1024,16]{0,1:T(8,128)S(1)} %select_reduce_fusion), channel_id=1, replica_groups=mesh['dp'=16,'tensor'=8] {'tensor'}, use_global_device_ids=true, to_apply=%region_4.5 | all-reduce | flops 16384 | bytes 98304 | tf_op jit(solution)/shard_map/psum | solution.py:98
  263.7 8.5 %convolution_convert_fusion = bf16[1024,128]{1,0:T(8,128)(2,1)S(1)} fusion(bf16[1024,8192]{1,0:T(8,128)(2,1)} %fusion.2, bf16[8192,128]{1,0:T(8,128)(2,1)S(1)} %copy-done), kind=kOutput, calls=%fused_computation.38 | convolution fusion | flops 2147614720 | bytes 19136512 | tf_op jit(solution)/shard_map/dot_general | solution.py:123
  272.2 2.4 copy-done.3
  274.6 0.6 copy-done.11
  275.2 4.5 %fusion.68 = f32[1024,128]{1,0:T(8,128)S(1)} fusion(bf16[1024,8192]{1,0:T(8,128)(2,1)S(1)} %copy-done.3, bf16[8192,128]{1,0:T(8,128)(2,1)S(1)} %copy-done.11), kind=kOutput, calls=%fused_computation.101 | convolution fusion | flops 2147483648 | bytes 19398656 | tf_op jit(solution)/shard_map/dot_general | solution.py:118
  279.7 0.1 all-gather.13.cloned.1.call-done
  279.8 5.4 %fusion.12 = bf16[1024,1024]{1,0:T(8,128)(2,1)S(1)} fusion(bf16[64,16,1024]{2,1,0:T(8,128)(2,1)} %all-gather.13.cloned.1.call-done, bf16[1024,16]{0,1:T(8,128)(2,1)S(1)} %psum.7, bf16[1024,64]{0,1:T(8,128)(2,1)S(1)} %get-tuple-element.22), kind=kOutput, calls=%fused_computation.23 | convolution fusion | flops 2150629376 | bytes 4358144 | tf_op jit(solution)/shard_map/dot_general | solution.py:105
  285.3 22.6 %add_bitcast_fusion = f32[128,8,8,128]{3,1,2,0:T(8,128)S(1)} fusion(bf16[1024,1024]{1,0:T(8,128)(2,1)S(1)} %fusion.12, bf16[1024,8192]{1,0:T(8,128)(2,1)} %fusion.2, bf16[8192,1024]{1,0:T(8,128)(2,1)} %param.16), kind=kOutput, calls=%fused_computation.26 | convolution fusion | flops 17181966336 | bytes 39845888 | tf_op jit(solution)/shard_map/dot_general | solution.py:112
  307.9 1.0 copy.82
  308.9 4.6 %fusion.66 = (f32[8,128,8,64]{3,2,1,0:T(8,128)}, f32[8,128,8,64]{3,2,1,0:T(8,128)}) fusion(f32[8,128,8,128]{3,2,1,0:T(8,128)S(1)} %bitcast.99), kind=kLoop, calls=%fused_computation.99 | loop fusion | bytes 8388608 | tf_op jit(solution)/shard_map/slice | solution.py:23
  313.4 0.2 subtract_convert_fusion.1
  313.7 0.3 broadcast_select_fusion.1
  314.0 0.8 copy.65
  314.9 5.2 %subtract_convert_fusion = (bf16[8,128,8,64]{3,1,2,0:T(8,128)(2,1)S(1)}, bf16[8,128,8,64]{3,1,2,0:T(8,128)(2,1)S(1)}) fusion(f32[8,128,8,64]{3,2,1,0:T(8,128)} %get-tuple-element.15, f32[8,128,8,64]{3,2,1,0:T(8,128)} %get-tuple-element.14, f32[128,64]{1,0:T(8,128)S(1)} %get-tuple-element.29, f32[128,64]{1,0:T(8,128)S(1)} %get-tuple-element.28), kind=kLoop, calls=%fused_computation.25 | loop fusion | flops 4194304 | bytes 6356992 | tf_op jit(solution)/shard_map/convert.4
  320.1 3.1 fusion.4
  323.2 0.0 copy-start.8
  323.2 3.2 fusion.3
  326.5 5.3 %fusion.11 = bf16[8,1,128,8,128]{4,2,3,0,1:T(8,128)(2,1)} fusion(f32[8,8,128]{2,1,0:T(8,128)S(1)} %fusion.3, f32[8,8,128]{2,1,0:T(8,128)S(1)} %get-tuple-element.30, f32[8,384,128,8]{2,1,3,0:T(8,128)S(1)} %get-tuple-element.31, pred[128,384]{0,1:T(8,128)(4,1)S(1)} %fusion.48, pred[8,128]{1,0:T(8,128)(4,1)S(1)} %copy-done.9, ...), kind=kOutput, calls=%fused_computation.21 | convolution fusion | flops 824705024 | bytes 15582208 | tf_op jit(solution)/shard_map/bkgts,bskd->btkgd/dot_general | solution.py:147
  331.7 4.1 %copy.73 = bf16[8,128,1024]{2,1,0:T(8,128)(2,1)} copy(bf16[8,128,1024]{1,2,0:T(8,128)(2,1)} %bitcast.103) | data formatting | bytes 4194304
  335.8 0.3 maximum_select_fusion.1
  336.1 0.1 maximum_bitcast_fusion.4
  336.2 0.1 broadcast_in_dim.108
  336.3 0.9 scatter_fusion
  337.2 0.0 copy-start.6
  337.2 0.8 copy-done.6
  (34 shorter events, 0.1 us)
Async XLA Ops:
  7.2 44.3 %copy-start = (bf16[8192,128]{1,0:T(8,128)(2,1)S(1)}, bf16[8192,128]{1,0:T(8,128)(2,1)}, u32[]{:S(2)}) copy-start(bf16[8192,128]{1,0:T(8,128)(2,1)} %param.18) | copy-start | bytes 6291460
  7.2 37.2 %all-gather.15.cloned.1.call-start = ((), (), s32[]{:S(2)}) async-start(), calls=%async_computation.4 | async-start | bytes 4718592 | tf_op jit(solution)/shard_map/all_gather | solution.py:65
  7.9 91.5 %all-gather.7.cloned.1.call-start = ((), (), s32[]{:S(2)}) async-start(), calls=%async_computation | async-start | bytes 2228224 | tf_op jit(solution)/shard_map/all_gather | solution.py:85
  44.3 3.4 %copy-start.4 = (bf16[1,256,8192]{2,1,0:T(8,128)(2,1)S(1)}, bf16[1,256,8192]{2,1,0:T(8,128)(2,1)}, u32[]{:S(2)}) copy-start(bf16[1,256,8192]{2,1,0:T(8,128)(2,1)} %all-gather.15.cloned.1.call-done) | copy-start | bytes 12582916
  51.5 4.6 %copy-start.12 = (s32[64]{0:T(128)S(1)}, s32[64]{0:T(128)}, u32[]{:S(2)}) copy-start(s32[64]{0:T(128)} %param.21) | copy-start | bytes 772
  51.5 4.6 %copy-start.13 = (s32[8]{0:T(128)S(1)}, s32[8]{0:T(128)}, u32[]{:S(2)}) copy-start(s32[8]{0:T(128)} %param.22) | copy-start | bytes 100
  51.5 5.2 %copy-start.14 = (s32[8]{0:T(128)S(1)}, s32[8]{0:T(128)}, u32[]{:S(2)}) copy-start(s32[8]{0:T(128)} %param.24) | copy-start | bytes 100
  51.5 5.8 %copy-start.15 = (s32[8]{0:T(128)S(1)}, s32[8]{0:T(128)}, u32[]{:S(2)}) copy-start(s32[8]{0:T(128)} %param.23) | copy-start | bytes 100
  51.5 6.6 %copy-start.16 = (s32[8,1]{0,1:T(1,128)S(1)}, s32[8,1]{0,1:T(1,128)}, u32[]{:S(2)}) copy-start(s32[8,1]{0,1:T(1,128)} %param.25) | copy-start | bytes 100
  54.1 131.3 %all-gather.9.cloned.1.call-start = ((), (), s32[]{:S(2)}) async-start(), calls=%async_computation.1 | async-start | bytes 18874368 | tf_op jit(solution)/shard_map/all_gather | solution.py:64
  54.8 178.5 %all-gather.11.cloned.1.call-start = ((), (), s32[]{:S(2)}) async-start(), calls=%async_computation.2 | async-start | bytes 2228224 | tf_op jit(solution)/shard_map/all_gather | solution.py:93
  55.4 224.4 %all-gather.13.cloned.1.call-start = ((), (), s32[]{:S(2)}) async-start(), calls=%async_computation.3 | async-start | bytes 2228224 | tf_op jit(solution)/shard_map/all_gather | solution.py:99
  185.4 10.7 %copy-start.2 = (bf16[1024,8192]{1,0:T(8,128)(2,1)S(1)}, bf16[1024,8192]{1,0:T(8,128)(2,1)}, u32[]{:S(2)}) copy-start(bf16[1024,8192]{1,0:T(8,128)(2,1)} %all-gather.9.cloned.1.call-done) | copy-start | bytes 50331652
  263.7 10.9 %copy-start.3 = (bf16[1024,8192]{1,0:T(8,128)(2,1)S(1)}, bf16[1024,8192]{1,0:T(8,128)(2,1)}, u32[]{:S(2)}) copy-start(bf16[1024,8192]{1,0:T(8,128)(2,1)} %fusion.2) | copy-start | bytes 50331652
  263.7 11.5 %copy-start.11 = (bf16[8192,128]{1,0:T(8,128)(2,1)S(1)}, bf16[8192,128]{1,0:T(8,128)(2,1)}, u32[]{:S(2)}) copy-start(bf16[8192,128]{1,0:T(8,128)(2,1)} %param.17) | copy-start | bytes 6291460
  308.9 4.8 %copy-start.9 = (pred[8,128]{1,0:T(8,128)(4,1)S(1)}, pred[8,128]{1,0:T(8,128)(4,1)}, u32[]{:S(2)}) copy-start(pred[8,128]{1,0:T(8,128)(4,1)} %iota_compare_fusion.3) | copy-start | bytes 3076
  314.9 5.2 %copy-start.5 = (bf16[8,256,1,128]{3,1,0,2:T(8,128)(2,1)S(1)}, bf16[8,256,1,128]{3,1,0,2:T(8,128)(2,1)}, u32[]{:S(2)}) copy-start(bf16[8,256,1,128]{3,1,0,2:T(8,128)(2,1)} %get-tuple-element.17) | copy-start | bytes 1572868
  323.2 3.2 copy-start.7
  323.2 3.2 copy-start.8
  331.7 4.6 %copy-start.10 = (s32[8]{0:T(128)S(1)}, s32[8]{0:T(128)}, u32[]{:S(2)}) copy-start(s32[8]{0:T(128)} %fusion.59) | copy-start | bytes 100
  331.7 6.2 %copy-start.1 = (bf16[8192,128]{1,0:T(8,128)(2,1)S(1)}, bf16[8192,128]{1,0:T(8,128)(2,1)}, u32[]{:S(2)}) copy-start(bf16[8192,128]{1,0:T(8,128)(2,1)} %param.18) | copy-start | bytes 6291460
  337.2 0.8 copy-start.6
Sparse Core Ops, SparseCore 0:
  9.7 34.5 all-gather.14
  54.2 45.1 all-gather.6
  101.1 84.1 all-gather.8
  187.4 45.8 all-gather.10
  235.3 44.5 all-gather.12
where the time goes:
time: 345 us
  waiting for transfers between devices  188 us (54%)
  matrix products  59.5 us (17%)
  other arithmetic  31.9 us (9%)
  blocking collectives  25.3 us (7%)
  local copies, waits for them, and re-layouts  25.1 us (7%)
  between operations  14.2 us (4%)
    all_gather x1, waiting for transfers between devices, on_device(): lax.all_gather(tokens.reshape(token_rows, d_part), 'tensor', axis=1, tile...  80.4 us
    all_gather x1, waiting for transfers between devices, on_device(): lax.all_gather(jnp.stack([pre_keys, pre_vals], 1), 'dp', axis=0, tiled=True)  40.8 us
    all_gather x1, waiting for transfers between devices, on_device(): lax.all_gather(shared_prefix_tokens.reshape(grp_dev * pre_len, d_part), '...  35.6 us
    all_gather x1, waiting for transfers between devices, on_device(): page_piece = lax.all_gather(adapter_down_weight, 'dp', axis=0, tiled=True)  29 us
    psum x1, blocking collectives, on_device(): low_rank_rows = lax.psum(partial_low, 'tensor').astype(jnp.bfloat16)  25.3 us
    dot_general x1, matrix products, on_device(): jnp.dot(normed_input, query_weight, preferred_element_type=jnp.float32)  22.6 us
    unnamed x37, local copies, waits for them, and re-layouts  14.3 us
    reduce_sum x2, other arithmetic, normalize(): scale = lax.rsqrt(jnp.mean(values * values, axis=-1, keepdims=True) + EPS)  10.7 us
  transfers between devices with their start and end apart: 5, of which 5 were waited for; matrix products, arithmetic and copies ran while one was open for 12% of the time, Pallas kernels for 0%

commit v1 on v0

--- a/solution.py
+++ b/solution.py
@@ -1,3 +1,4 @@
+import functools
 import jax
 import jax.numpy as jnp
 from jax import lax
@@ -9,6 +10,14 @@
 EPS = 1e-05
 THETA = 500000.0
 ADAPTER_SCALE = 2.0
+
+
+def build_results(original, a_name):
+    response = lax.all_gather(original, a_name)
+    return jnp.sum(response, axis=0)
+
+
+push_zone = functools.partial(build_results, a_name="tensor")
 
 
 def rope_tables(positions, width):
@@ -95,7 +104,7 @@
     part = jnp.einsum("td,ndr->tnr", local_rows, page_piece, preferred_element_type=jnp.float32)
     pick = row_slot[:, None] == jnp.arange(count)[None, :]
     partial_low = jnp.sum(jnp.where(pick[:, :, None], part, 0.0), axis=1)
-    low_rank_rows = lax.psum(partial_low, "tensor").astype(jnp.bfloat16)
+    low_rank_rows = push_zone(partial_low).astype(jnp.bfloat16)
     page_piece = lax.all_gather(adapter_up_weight, "dp", axis=0, tiled=True)
     count = page_piece.shape[0]
     pick = (row_slot[:, None] == jnp.arange(count)[None, :]).astype(jnp.bfloat16)

time: 345 us -> 361 us (1.046); the launches traced: 345 us -> 354 us
  waiting for transfers between devices: 188 us -> 206 us
  blocking collectives: 25.3 us -> 14 us
  matrix products: 59.5 us -> 65.4 us
    psum x1 -> x0, blocking collectives: 25.3 us -> none  [on_device(): low_rank_rows = lax.psum(partial_low, 'tensor').astype(jnp.bfloat16)]
    all_gather x1, waiting for transfers between devices: 0.15 us -> 17.9 us  [on_device(): page_piece = lax.all_gather(adapter_up_weight, 'dp', axis=0, tiled=True)]
    all_gather x0 -> x1, blocking collectives: none -> 14 us  [build_results(): response = lax.all_gather(original, a_name)]
    dot_general x1, matrix products: 22.6 us -> 32.4 us  [on_device(): jnp.dot(normed_input, query_weight, preferred_element_type=jnp.float32)]
    dot_general x1, matrix products: 8.46 us -> 4.5 us  [on_device(): jnp.dot(normed_input, value_weight, preferred_element_type=jnp.float32)]
    unnamed x37 -> x38, local copies, waits for them, and re-layouts: 14.3 us -> 11.6 us
  transfers between devices with their start and end apart: 5 -> 5, of which waited for: 5 -> 5; matrix products, arithmetic and copies ran while one was open for 12% -> 11% of each run, Pallas kernels for 0% -> 0%
where the time goes in v1:
time: 361 us; the launch traced here: 354 us
  waiting for transfers between devices  206 us (57%)
  matrix products  65.4 us (18%)
  other arithmetic  32 us (9%)
  local copies, waits for them, and re-layouts  22.4 us (6%)
  between operations  14.4 us (4%)
  blocking collectives  14 us (4%)
    all_gather x1, waiting for transfers between devices, on_device(): lax.all_gather(tokens.reshape(token_rows, d_part), 'tensor', axis=1, tile...  80.4 us
    all_gather x1, waiting for transfers between devices, on_device(): lax.all_gather(jnp.stack([pre_keys, pre_vals], 1), 'dp', axis=0, tiled=True)  40.8 us
    all_gather x1, waiting for transfers between devices, on_device(): lax.all_gather(shared_prefix_tokens.reshape(grp_dev * pre_len, d_part), '...  35.6 us
    dot_general x1, matrix products, on_device(): jnp.dot(normed_input, query_weight, preferred_element_type=jnp.float32)  32.4 us
    all_gather x1, waiting for transfers between devices, on_device(): page_piece = lax.all_gather(adapter_down_weight, 'dp', axis=0, tiled=True)  29 us
    all_gather x1, waiting for transfers between devices, on_device(): page_piece = lax.all_gather(adapter_up_weight, 'dp', axis=0, tiled=True)  17.9 us
    all_gather x1, blocking collectives, build_results(): response = lax.all_gather(original, a_name)  14 us
    unnamed x38, local copies, waits for them, and re-layouts  11.6 us
  transfers between devices with their start and end apart: 5, of which 5 were waited for; matrix products, arithmetic and copies ran while one was open for 11% of the time, Pallas kernels for 0%

profile of v1, /device:TPU:0, one launch (start us, length us, event | category | flops | bytes accessed | tf_op | source)
XLA Modules:
  0.0 354.4 jit_solution(11165510129076116435)
XLA Ops:
  7.2 0.0 copy-start
  7.2 0.0 all-gather.16.cloned.1.call-start
  7.2 0.7 all-gather.16.cloned.1.call-update
  7.9 0.0 all-gather.8.cloned.1.call-start
  8.0 0.7 convert_element_type.118
  8.7 35.6 %all-gather.16.cloned.1.call-done = bf16[1,256,8192]{2,1,0:T(8,128)(2,1)} async-done(((bf16[1,256,1024]{2,1,0:T(8,128)(2,1)}), bf16[1,256,8192]{2,1,0:T(8,128)(2,1)}) %all-gather.16.cloned.1.call-update) | async-done | bytes 4194320 | tf_op jit(solution)/shard_map/all_gather | solution.py:74
  44.3 3.3 fusion.5
  47.6 0.2 copy-done.4
  47.8 3.3 fusion.33
  51.1 0.3 fusion.58
  51.5 0.0 copy-start.14
  51.5 0.0 copy-start.15
  51.5 1.7 fusion.39
  53.3 0.8 copy.63
  54.1 0.0 all-gather.8.cloned.1.call-update
  54.1 0.0 all-gather.10.cloned.1.call-start
  54.1 0.7 all-gather.10.cloned.1.call-update
  54.8 0.0 all-gather.12.cloned.1.call-start
  54.9 0.5 all-gather.12.cloned.1.call-update
  55.4 0.0 all-gather.14.cloned.1.call-start
  55.4 0.5 all-gather.14.cloned.1.call-update
  56.0 0.2 select_reduce_fusion.1
  56.2 0.1 broadcast_bitcast_fusion
  56.3 0.1 fusion.65
  56.4 0.3 multiply_cosine_fusion
  56.7 0.6 iota_compare_fusion.3
  57.3 0.6 pad_clamp_fusion
  57.9 0.2 fusion.48
  58.1 0.5 fusion.59
  58.6 40.8 %all-gather.8.cloned.1.call-done = bf16[16,2,256,128]{3,2,1,0:T(8,128)(2,1)} async-done(((bf16[1,2,256,128]{3,2,1,0:T(8,128)(2,1)}), bf16[16,2,256,128]{3,2,1,0:T(8,128)(2,1)}) %all-gather.8.cloned.1.call-update) | async-done | bytes 2097168 | tf_op jit(solution)/shard_map/all_gather | solution.py:94
  99.4 2.5 gather_fusion
  101.9 1.0 fusion.67
  102.9 2.0 copy.78
  105.0 80.4 %all-gather.10.cloned.1.call-done = bf16[1024,8192]{1,0:T(8,128)(2,1)} async-done(((bf16[1024,1024]{1,0:T(8,128)(2,1)}), bf16[1024,8192]{1,0:T(8,128)(2,1)}) %all-gather.10.cloned.1.call-update) | async-done | bytes 16777232 | tf_op jit(solution)/shard_map/all_gather | solution.py:73
  185.4 7.5 %fusion = f32[1024]{0:T(1024)S(1)} fusion(bf16[1024,8192]{1,0:T(8,128)(2,1)} %all-gather.10.cloned.1.call-done), kind=kLoop, calls=%fused_computation.4 | loop fusion | flops 25164800 | bytes 16781312 | tf_op jit(solution)/shard_map/reduce_sum | solution.py:43
  192.9 3.2 copy-done.2
  196.0 8.3 %fusion.2 = bf16[1024,8192]{1,0:T(8,128)(2,1)} fusion(bf16[1024,8192]{1,0:T(8,128)(2,1)S(1)} %copy-done.2, f32[8192]{0:T(1024)S(1)} %convert_element_type.118, f32[1024]{0:T(1024)S(1)} %add_rsqrt_fusion), kind=kLoop, calls=%fused_computation.6 | loop fusion | flops 33554432 | bytes 33591296 | tf_op jit(solution)/shard_map/convert_element_type | solution.py:44
  204.3 29.0 %all-gather.12.cloned.1.call-done = bf16[64,1024,16]{1,2,0:T(8,128)(2,1)} async-done(((bf16[4,1024,16]{1,2,0:T(8,128)(2,1)}), bf16[64,1024,16]{1,2,0:T(8,128)(2,1)}) %all-gather.12.cloned.1.call-update) | async-done | bytes 2097168 | tf_op jit(solution)/shard_map/all_gather | solution.py:102
  233.3 5.2 %select_reduce_fusion = f32[1024,16]{0,1:T(8,128)S(1)} fusion(pred[1024,64]{0,1:T(8,128)(4,1)S(1)} %get-tuple-element.23, bf16[64,1024,16]{1,2,0:T(8,128)(2,1)} %all-gather.12.cloned.1.call-done, bf16[1024,8192]{1,0:T(8,128)(2,1)} %fusion.2, s32[]{:T(128)S(6)} %select_n.72), kind=kOutput, calls=%fused_computation.27 | convolution fusion | flops 2149564416 | bytes 4325380 | tf_op jit(solution)/shard_map/td,ndr->tnr/dot_general | solution.py:104
  238.5 14.0 %all-gather.1 = f32[8192,16]{0,1:T(8,128)S(1)} all-gather(f32[1024,16]{0,1:T(8,128)S(1)} %select_reduce_fusion), channel_id=3, replica_groups=mesh['dp'=16,'tensor'=8] {'tensor'}, dimensions={0}, use_global_device_ids=true | all-gather | bytes 589824 | tf_op jit(solution)/shard_map/all_gather | solution.py:16
  252.5 0.3 copy.82
  252.8 0.1 bitcast_reduce_fusion
  253.0 0.0 copy-start.11
  253.0 4.5 %convolution_convert_fusion = bf16[1024,128]{1,0:T(8,128)(2,1)S(1)} fusion(bf16[1024,8192]{1,0:T(8,128)(2,1)S(1)} %copy-done.3, bf16[8192,128]{1,0:T(8,128)(2,1)S(1)} %copy-done), kind=kOutput, calls=%fused_computation.38 | convolution fusion | flops 2147614720 | bytes 19136512 | tf_op jit(solution)/shard_map/dot_general | solution.py:132
  257.5 4.5 %fusion.68 = f32[1024,128]{1,0:T(8,128)S(1)} fusion(bf16[1024,8192]{1,0:T(8,128)(2,1)S(1)} %copy-done.3, bf16[8192,128]{1,0:T(8,128)(2,1)S(1)} %copy-done.11), kind=kOutput, calls=%fused_computation.102 | convolution fusion | flops 2147483648 | bytes 19398656 | tf_op jit(solution)/shard_map/dot_general | solution.py:127
  262.0 17.9 %all-gather.14.cloned.1.call-done = bf16[64,16,1024]{2,1,0:T(8,128)(2,1)} async-done(((bf16[4,16,1024]{2,1,0:T(8,128)(2,1)}), bf16[64,16,1024]{2,1,0:T(8,128)(2,1)}) %all-gather.14.cloned.1.call-update) | async-done | bytes 2097168 | tf_op jit(solution)/shard_map/all_gather | solution.py:108
  279.8 5.4 %fusion.12 = bf16[1024,1024]{1,0:T(8,128)(2,1)S(1)} fusion(bf16[64,16,1024]{2,1,0:T(8,128)(2,1)} %all-gather.14.cloned.1.call-done, bf16[1024,16]{0,1:T(8,128)(2,1)S(1)} %bitcast_reduce_fusion, bf16[1024,64]{0,1:T(8,128)(2,1)S(1)} %get-tuple-element.22), kind=kOutput, calls=%fused_computation.23 | convolution fusion | flops 2150629376 | bytes 4358144 | tf_op jit(solution)/shard_map/dot_general | solution.py:114
  285.3 32.4 %add_bitcast_fusion = f32[128,8,8,128]{3,1,2,0:T(8,128)S(1)} fusion(bf16[1024,1024]{1,0:T(8,128)(2,1)S(1)} %fusion.12, bf16[1024,8192]{1,0:T(8,128)(2,1)} %fusion.2, bf16[8192,1024]{1,0:T(8,128)(2,1)} %param.16), kind=kOutput, calls=%fused_computation.26 | convolution fusion | flops 17181966336 | bytes 39845888 | tf_op jit(solution)/shard_map/dot_general | solution.py:121
  317.7 1.0 copy.83
  318.7 4.6 %fusion.66 = (f32[8,128,8,64]{3,2,1,0:T(8,128)}, f32[8,128,8,64]{3,2,1,0:T(8,128)}) fusion(f32[8,128,8,128]{3,2,1,0:T(8,128)S(1)} %bitcast.104), kind=kLoop, calls=%fused_computation.100 | loop fusion | bytes 8388608 | tf_op jit(solution)/shard_map/slice | solution.py:32
  323.2 0.2 subtract_convert_fusion.1
  323.5 0.3 broadcast_select_fusion.1
  323.8 0.8 copy.65
  324.7 5.2 %subtract_convert_fusion = (bf16[8,128,8,64]{3,1,2,0:T(8,128)(2,1)S(1)}, bf16[8,128,8,64]{3,1,2,0:T(8,128)(2,1)S(1)}) fusion(f32[8,128,8,64]{3,2,1,0:T(8,128)} %get-tuple-element.15, f32[8,128,8,64]{3,2,1,0:T(8,128)} %get-tuple-element.14, f32[128,64]{1,0:T(8,128)S(1)} %get-tuple-element.29, f32[128,64]{1,0:T(8,128)S(1)} %get-tuple-element.28), kind=kLoop, calls=%fused_computation.25 | loop fusion | flops 4194304 | bytes 6356992 | tf_op jit(solution)/shard_map/convert.4
  329.9 3.1 fusion.4
  333.0 0.0 copy-start.8
  333.0 3.2 fusion.3
  336.2 5.2 %fusion.11 = bf16[8,1,128,8,128]{4,2,3,0,1:T(8,128)(2,1)} fusion(f32[8,8,128]{2,1,0:T(8,128)S(1)} %fusion.3, f32[8,8,128]{2,1,0:T(8,128)S(1)} %get-tuple-element.30, f32[8,384,128,8]{2,1,3,0:T(8,128)S(1)} %get-tuple-element.31, pred[128,384]{0,1:T(8,128)(4,1)S(1)} %fusion.48, pred[8,128]{1,0:T(8,128)(4,1)S(1)} %copy-done.9, ...), kind=kOutput, calls=%fused_computation.21 | convolution fusion | flops 824705024 | bytes 15582208 | tf_op jit(solution)/shard_map/bkgts,bskd->btkgd/dot_general | solution.py:156
  341.5 4.1 %copy.73 = bf16[8,128,1024]{2,1,0:T(8,128)(2,1)} copy(bf16[8,128,1024]{1,2,0:T(8,128)(2,1)} %bitcast.108) | data formatting | bytes 4194304
  345.5 0.3 maximum_select_fusion.1
  345.8 0.1 maximum_bitcast_fusion.4
  345.9 0.1 broadcast_in_dim.108
  346.0 0.9 scatter_fusion
  346.9 0.8 copy-done.6
  (36 shorter events, 0.2 us)
Async XLA Ops:
  7.2 44.3 %copy-start = (bf16[8192,128]{1,0:T(8,128)(2,1)S(1)}, bf16[8192,128]{1,0:T(8,128)(2,1)}, u32[]{:S(2)}) copy-start(bf16[8192,128]{1,0:T(8,128)(2,1)} %param.18) | copy-start | bytes 6291460
  7.2 37.2 %all-gather.16.cloned.1.call-start = ((), (), s32[]{:S(2)}) async-start(), calls=%async_computation.4 | async-start | bytes 4718592 | tf_op jit(solution)/shard_map/all_gather | solution.py:74
  7.9 91.5 %all-gather.8.cloned.1.call-start = ((), (), s32[]{:S(2)}) async-start(), calls=%async_computation | async-start | bytes 2228224 | tf_op jit(solution)/shard_map/all_gather | solution.py:94
  44.3 3.4 copy-start.4
  51.5 4.6 %copy-start.12 = (s32[64]{0:T(128)S(1)}, s32[64]{0:T(128)}, u32[]{:S(2)}) copy-start(s32[64]{0:T(128)} %param.21) | copy-start | bytes 772
  51.5 4.6 %copy-start.13 = (s32[8]{0:T(128)S(1)}, s32[8]{0:T(128)}, u32[]{:S(2)}) copy-start(s32[8]{0:T(128)} %param.22) | copy-start | bytes 100
  51.5 5.2 %copy-start.14 = (s32[8]{0:T(128)S(1)}, s32[8]{0:T(128)}, u32[]{:S(2)}) copy-start(s32[8]{0:T(128)} %param.24) | copy-start | bytes 100
  51.5 5.8 %copy-start.15 = (s32[8]{0:T(128)S(1)}, s32[8]{0:T(128)}, u32[]{:S(2)}) copy-start(s32[8]{0:T(128)} %param.23) | copy-start | bytes 100
  51.5 6.6 %copy-start.16 = (s32[8,1]{0,1:T(1,128)S(1)}, s32[8,1]{0,1:T(1,128)}, u32[]{:S(2)}) copy-start(s32[8,1]{0,1:T(1,128)} %param.25) | copy-start | bytes 100
  54.1 131.3 %all-gather.10.cloned.1.call-start = ((), (), s32[]{:S(2)}) async-start(), calls=%async_computation.1 | async-start | bytes 18874368 | tf_op jit(solution)/shard_map/all_gather | solution.py:73
  54.8 178.5 %all-gather.12.cloned.1.call-start = ((), (), s32[]{:S(2)}) async-start(), calls=%async_computation.2 | async-start | bytes 2228224 | tf_op jit(solution)/shard_map/all_gather | solution.py:102
  55.4 224.4 %all-gather.14.cloned.1.call-start = ((), (), s32[]{:S(2)}) async-start(), calls=%async_computation.3 | async-start | bytes 2228224 | tf_op jit(solution)/shard_map/all_gather | solution.py:108
  185.4 10.7 %copy-start.2 = (bf16[1024,8192]{1,0:T(8,128)(2,1)S(1)}, bf16[1024,8192]{1,0:T(8,128)(2,1)}, u32[]{:S(2)}) copy-start(bf16[1024,8192]{1,0:T(8,128)(2,1)} %all-gather.10.cloned.1.call-done) | copy-start | bytes 50331652
  233.3 19.7 %copy-start.3 = (bf16[1024,8192]{1,0:T(8,128)(2,1)S(1)}, bf16[1024,8192]{1,0:T(8,128)(2,1)}, u32[]{:S(2)}) copy-start(bf16[1024,8192]{1,0:T(8,128)(2,1)} %fusion.2) | copy-start | bytes 50331652
  253.0 4.5 %copy-start.11 = (bf16[8192,128]{1,0:T(8,128)(2,1)S(1)}, bf16[8192,128]{1,0:T(8,128)(2,1)}, u32[]{:S(2)}) copy-start(bf16[8192,128]{1,0:T(8,128)(2,1)} %param.17) | copy-start | bytes 6291460
  318.7 4.8 %copy-start.9 = (pred[8,128]{1,0:T(8,128)(4,1)S(1)}, pred[8,128]{1,0:T(8,128)(4,1)}, u32[]{:S(2)}) copy-start(pred[8,128]{1,0:T(8,128)(4,1)} %iota_compare_fusion.3) | copy-start | bytes 3076
  324.7 5.2 %copy-start.5 = (bf16[8,256,1,128]{3,1,0,2:T(8,128)(2,1)S(1)}, bf16[8,256,1,128]{3,1,0,2:T(8,128)(2,1)}, u32[]{:S(2)}) copy-start(bf16[8,256,1,128]{3,1,0,2:T(8,128)(2,1)} %get-tuple-element.17) | copy-start | bytes 1572868
  333.0 3.2 copy-start.7
  333.0 3.2 copy-start.8
  341.5 4.6 %copy-start.10 = (s32[8]{0:T(128)S(1)}, s32[8]{0:T(128)}, u32[]{:S(2)}) copy-start(s32[8]{0:T(128)} %fusion.59) | copy-start | bytes 100
  341.5 6.2 %copy-start.1 = (bf16[8192,128]{1,0:T(8,128)(2,1)S(1)}, bf16[8192,128]{1,0:T(8,128)(2,1)}, u32[]{:S(2)}) copy-start(bf16[8192,128]{1,0:T(8,128)(2,1)} %param.18) | copy-start | bytes 6291460
  346.9 0.8 copy-start.6
Sparse Core Ops, SparseCore 0:
  9.7 34.5 all-gather.15
  54.2 45.1 all-gather.7
  101.1 84.1 all-gather.9
  187.4 45.8 all-gather.11
  235.3 44.5 all-gather.13
